TPU v7x, 128 devices: a whole 4x4x4 slice. The times are simulated.
128 devices in a mesh: grp: 4 (over x), row: 32 (over z, y, core).
Axes of the slice: x: 4, y: 4, z: 4, core: 2. Of those that a mesh axis runs over, the one named last changes fastest.
Arguments:
- vectors: bfloat16 [524288, 1024], P(('grp', 'row')), may hold values from -6 to 6
- keep_bits: int32 [524288], P(('grp', 'row')), may hold values 0 or 1
- counts: int32 [4096], P(('grp', 'row')), may hold values from 1 to 128
- block_list: int32 [4096], replicated, may hold values from 0 to 2047, as said below
- home_pos: int32 [2048], replicated, may hold values from 0 to 2047, as said below
- old_centroids: bfloat16 [2048, 1024], P('grp'), may hold values from -1.5 to 1.5
Outputs:
- new_centroids: bfloat16 [2048, 1024], P(('grp', 'row'))
- scores: float32 [524288, 512], P(('grp', 'row'))
Inputs may be any that keep to these rules, and one draw needn't show every extreme that they name: `block_list`: every block's list is one of the lists of the block's own group; on one device at most one block has a list whose new position lies in any given other group, and this most is reached in every draw. `home_pos`: A permutation of the positions; position p lies in group p // 512.
All inputs are finite; a program needn't handle non-finite values. No bound on the sum of `keep_bits` on one device may be relied on, other than what follows from the above.
Results may differ from a plain program's by a relative error of at most 0.002.
Values may be sent and summed in bfloat16 or wider, within the bound.
A program may use at most 128 MiB of HBM per device.

v0:
```python
import math

import jax
import jax.numpy as jnp
from jax import lax
from jax.sharding import PartitionSpec as P

PRIOR = 16


def centroid_rows(sums, totals, previous):
    prior_weight = 1.0 * PRIOR
    return (
        (sums + prior_weight * previous.astype(jnp.float32)) / (totals + prior_weight)[:, None]
    ).astype(jnp.bfloat16)


def score_rows(rows, table, norms, factor):
    dots = lax.dot_general(
        rows, table, (((1,), (1,)), ((), ())), preferred_element_type=jnp.float32
    )
    return (2.0 * dots - norms[None, :]) * factor


def local(vectors, keep_bits, counts, block_list, home_pos, old_centroids):
    n_groups = lax.axis_size("grp")
    n_rows = lax.axis_size("row")
    group_index = lax.axis_index("grp")
    row_index = lax.axis_index("row")
    blocks = counts.shape[0]
    block_rows = vectors.shape[0] // blocks
    width = vectors.shape[1]
    lists_group = old_centroids.shape[0]
    factor = 1.0 / math.sqrt(width)
    row_blocks = vectors.reshape(blocks, block_rows, width)
    position = lax.broadcasted_iota(jnp.int32, (blocks, block_rows), 1)
    alive = (
        keep_bits.reshape(blocks, block_rows) * (position < counts[:, None]).astype(jnp.int32)
    ).astype(jnp.float32)
    alive_half = alive.astype(jnp.bfloat16)
    masked = row_blocks * alive_half[:, :, None]
    homes = jnp.take(home_pos, block_list)
    home_groups = (homes // lists_group).reshape(n_groups, n_rows, blocks)
    home_slots = (homes % lists_group).reshape(n_groups, n_rows, blocks)
    peer_groups = lax.dynamic_index_in_dim(home_groups, row_index, 1, keepdims=False)
    peer_slots = lax.dynamic_index_in_dim(home_slots, row_index, 1, keepdims=False)
    mine_groups = lax.dynamic_index_in_dim(peer_groups, group_index, 0, keepdims=False)
    mine_slots = lax.dynamic_index_in_dim(peer_slots, group_index, 0, keepdims=False)
    staying = mine_groups == group_index
    block_sums = jnp.einsum(
        "bi,bid->bd", alive_half, row_blocks, preferred_element_type=jnp.float32
    )
    block_counts = jnp.sum(alive, axis=1)
    list_iota = lax.broadcasted_iota(jnp.int32, (lists_group, blocks), 0)
    stay_onehot = ((mine_slots[None, :] == list_iota) & staying[None, :]).astype(jnp.float32)
    sums = jnp.dot(
        stay_onehot, block_sums, precision=lax.Precision.HIGHEST, preferred_element_type=jnp.float32
    )
    totals = jnp.dot(
        stay_onehot,
        block_counts,
        precision=lax.Precision.HIGHEST,
        preferred_element_type=jnp.float32,
    )
    group_iota = lax.broadcasted_iota(jnp.int32, (n_groups, blocks), 0)
    outgoing = (mine_groups[None, :] == group_iota) & jnp.logical_not(staying)[None, :]
    present = jnp.any(outgoing, axis=1)
    pick_index = jnp.argmax(outgoing, axis=1)
    incoming = (peer_groups == group_index) & (group_iota != group_index)
    arriving = jnp.any(incoming, axis=1)
    arrive_index = jnp.argmax(incoming, axis=1)
    arrive_slots = jnp.take_along_axis(peer_slots, arrive_index[:, None], axis=1)[:, 0]
    slot_iota = lax.broadcasted_iota(jnp.int32, (lists_group, n_groups), 0)
    arrive_onehot = ((arrive_slots[None, :] == slot_iota) & arriving[None, :]).astype(jnp.float32)
    send_sums = jnp.take(block_sums, pick_index, axis=0) * present.astype(jnp.float32)[:, None]
    send_counts = jnp.take(block_counts, pick_index) * present.astype(jnp.float32)
    got_sums, got_counts = (
        lax.all_to_all(send_sums, "grp", split_axis=0, concat_axis=0, tiled=True),
        lax.all_to_all(send_counts, "grp", split_axis=0, concat_axis=0, tiled=True),
    )
    sums = sums + jnp.dot(
        arrive_onehot, got_sums, precision=lax.Precision.HIGHEST, preferred_element_type=jnp.float32
    )
    totals = totals + jnp.dot(
        arrive_onehot,
        got_counts,
        precision=lax.Precision.HIGHEST,
        preferred_element_type=jnp.float32,
    )
    share = lists_group // n_rows
    all_sums, all_totals = lax.psum((sums, totals), "row")
    table = centroid_rows(all_sums, all_totals, old_centroids)
    new_centroids = lax.dynamic_slice_in_dim(table, row_index * share, share, 0)
    tables = lax.all_gather(table, "grp", axis=0, tiled=True)
    all_norms = jnp.sum(jnp.square(tables.astype(jnp.float32)), axis=1)

    def one_block(item):
        rows, weights, group_of = item
        start = group_of * lists_group
        part = lax.dynamic_slice_in_dim(tables, start, lists_group, 0)
        part_norms = lax.dynamic_slice_in_dim(all_norms, start, lists_group, 0)
        return score_rows(rows, part, part_norms, factor) * weights[:, None]

    scores = lax.map(one_block, (masked, alive, mine_groups))
    return (new_centroids, scores.reshape(blocks * block_rows, lists_group))


def solution(mesh):
    in_specs = (
        P(("grp", "row"), None),
        P(("grp", "row")),
        P(("grp", "row")),
        P(),
        P(),
        P("grp", None),
    )
    out_specs = (P(("grp", "row"), None), P(("grp", "row"), None))
    return jax.shard_map(local, mesh=mesh, in_specs=in_specs, out_specs=out_specs, check_vma=False)
```

profile of v0, /device:TPU:1, one launch (start us, length us, event | category | flops | bytes accessed | tf_op | source)
XLA Modules:
  0.0 343.5 jit_solution(9335938980896367984)
XLA Ops:
  7.9 23.0 %gather_fusion = s32[4096]{0:T(1024)S(1)} fusion(s32[2048]{0:T(1024)S(1)} %copy-done, s32[4096]{0:T(1024)S(1)} %fusion.35), kind=kCustom, calls=%fused_computation | custom fusion | bytes 49152 | tf_op jit(solution)/shard_map/jit(_take)/gather | solution.py:42
  32.8 4.6 %fusion.33 = f32[32,1,1024]{2,1,0:T(1,128)S(1)} fusion(bf16[32,128,1024]{2,1,0:T(8,128)(2,1)} %bitcast.65, bf16[32,128,1]{1,0,2:T(8,128)(2,1)S(1)} %convert_bitcast_fusion), kind=kOutput, calls=%fused_computation.51 | convolution fusion | flops 8388608 | bytes 8527872 | tf_op jit(solution)/shard_map/bi,bid->bd/dot_general | solution.py:50
  38.7 4.8 %all-to-all-start = ((f32[4,1,1024]{2,1,0:T(1,128)}), f32[4,1,1024]{2,1,0:T(1,128)S(1)}, u32[]{:S(2)}, u32[]{:S(2)}) async-start(f32[4,1,1024]{2,1,0:T(1,128)} %copy.12), calls=%async_computation | async-start | bytes 32768 | tf_op jit(solution)/shard_map/all_to_all | solution.py:78
  50.8 3.2 all-to-all-start.1
  54.3 3.7 %all-to-all-done.1 = f32[4,1,1]{2,1,0:T(1,128)S(1)} async-done(((f32[4,1,1]{2,1,0:T(1,128)}), f32[4,1,1]{2,1,0:T(1,128)S(1)}, u32[]{:S(2)}, u32[]{:S(2)}) %all-to-all-start.1) | async-done | bytes 48 | tf_op jit(solution)/shard_map/all_to_all | solution.py:79
  58.4 66.9 %psum.15 = f32[512]{0:T(512)S(1)} all-reduce(f32[512]{0:T(512)S(1)} %add.82), channel_id=1, replica_groups=mesh['grp'=4,'row'=32] {'row'}, use_global_device_ids=true, to_apply=%region_6.7 | all-reduce | flops 512 | bytes 4096 | tf_op jit(solution)/shard_map/psum | solution.py:91
  125.3 34.9 %all-reduce.2.cloned.1.call-done = f32[512,1024]{1,0:T(8,128)} async-done(((f32[512,1024]{1,0:T(8,128)}), f32[512,1024]{1,0:T(8,128)}) %all-reduce.2.cloned.1.call-update) | async-done | bytes 2097168 | tf_op jit(solution)/shard_map/psum | solution.py:91
  160.1 3.1 divide_convert_fusion
  163.3 7.2 %broadcast_multiply_fusion = bf16[32,128,1024]{2,1,0:T(8,128)(2,1)} fusion(bf16[32,128,1024]{2,1,0:T(8,128)(2,1)} %bitcast.66, bf16[32,128]{1,0:T(8,128)(2,1)S(1)} %convert_element_type.35), kind=kLoop, calls=%fused_computation.17 | loop fusion | flops 4194304 | bytes 16785408 | tf_op jit(solution)/shard_map/mul | solution.py:41
  171.9 39.1 %all-gather.2.cloned.1.call-done = bf16[2048,1024]{1,0:T(8,128)(2,1)} async-done(((bf16[512,1024]{1,0:T(8,128)(2,1)}), bf16[2048,1024]{1,0:T(8,128)(2,1)}) %all-gather.2.cloned.1.call-update) | async-done | bytes 4194320 | tf_op jit(solution)/shard_map/all_gather | solution.py:94
  211.0 3.1 multiply_reduce_fusion
  214.1 122.6 %while.10 = (s32[]{:T(128)}, f32[32,128,512]{2,1,0:T(8,128)}, bf16[32,128,1024]{2,1,0:T(8,128)(2,1)}, s32[32]{0:T(128)S(1)}, bf16[2048,1024]{1,0:T(8,128)(2,1)},...) while((s32[]{:T(128)}, f32[32,128,512]{2,1,0:T(8,128)}, ...), condition=%wide.region_9.10_spmd, body=%wide.region_8.9_spmd.sunk | while | flops 134414464 | bytes 1582263 | solution.py:104
  219.3 2.5 fusion.56
  223.1 2.5 fusion.56
  226.9 2.5 fusion.56
  230.8 2.5 fusion.56
  234.6 2.5 fusion.56
  238.4 2.5 fusion.56
  242.2 2.5 fusion.56
  246.1 2.5 fusion.56
  249.9 2.5 fusion.56
  311.2 2.5 fusion.56
  315.0 2.5 fusion.56
  318.9 2.5 fusion.56
  (172 shorter events, 85.6 us)
Async XLA Ops:
  7.2 0.7 copy-start
  7.9 23.1 %copy-start.2 = (s32[4096]{0:T(1024)S(1)}, s32[4096]{0:T(1024)}, u32[]{:S(2)}) copy-start(s32[4096]{0:T(1024)} %param.11) | copy-start | bytes 49156
  7.9 24.0 %copy-start.3 = (s32[4096]{0:T(1024)S(1)}, s32[4096]{0:T(1024)}, u32[]{:S(2)}) copy-start(s32[4096]{0:T(1024)} %param.9) | copy-start | bytes 49156
  7.9 24.0 %copy-start.4 = (s32[32]{0:T(128)S(1)}, s32[32]{0:T(128)}, u32[]{:S(2)}) copy-start(s32[32]{0:T(128)} %param.10) | copy-start | bytes 388
  37.4 122.7 %copy-start.1 = (bf16[512,1024]{1,0:T(8,128)(2,1)S(1)}, bf16[512,1024]{1,0:T(8,128)(2,1)}, u32[]{:S(2)}) copy-start(bf16[512,1024]{1,0:T(8,128)(2,1)} %param.13) | copy-start | bytes 3145732
  38.7 9.0 %all-to-all-start = ((f32[4,1,1024]{2,1,0:T(1,128)}), f32[4,1,1024]{2,1,0:T(1,128)S(1)}, u32[]{:S(2)}, u32[]{:S(2)}) async-start(f32[4,1,1024]{2,1,0:T(1,128)} %copy.12), calls=%async_computation | async-start | bytes 32768 | tf_op jit(solution)/shard_map/all_to_all | solution.py:78
  43.5 116.6 %all-reduce.2.cloned.1.call-start = ((), (), s32[]{:S(2)}) async-start(), calls=%async_computation.2 | async-start | bytes 4194304 | tf_op jit(solution)/shard_map/psum | solution.py:91
  50.8 7.3 %all-to-all-start.1 = ((f32[4,1,1]{2,1,0:T(1,128)}), f32[4,1,1]{2,1,0:T(1,128)S(1)}, u32[]{:S(2)}, u32[]{:S(2)}) async-start(f32[4,1,1]{2,1,0:T(1,128)} %copy.13), calls=%async_computation.1 | async-start | bytes 4096 | tf_op jit(solution)/shard_map/all_to_all | solution.py:79
  54.0 157.0 %all-gather.2.cloned.1.call-start = ((), (), s32[]{:S(2)}) async-start(), calls=%async_computation.3 | async-start | bytes 5242880 | tf_op jit(solution)/shard_map/all_gather | solution.py:94
Sparse Core Ops, SparseCore 0:
  50.2 109.8 all-reduce.1
  163.4 47.5 all-gather.1
where the time goes:
time: 345 us; the launch traced here: 344 us
  matrix products  88.5 us (26%)
  waiting for transfers between devices  79.4 us (23%)
  blocking collectives  66.9 us (19%)
  local copies, waits for them, and re-layouts  49.8 us (14%)
  loops' own time  20 us (6%)
  other arithmetic  16.7 us (5%)
  between operations  14.2 us (4%)
  starting transfers between devices  8.1 us (2%)
    dot_general x32, matrix products, score_rows(): lax.dot_general(rows, table, (((1,), (1,)), ((), ())), preferred_element_...  80.2 us
    psum x1, blocking collectives, local(): all_sums, all_totals = lax.psum((sums, totals), 'row')  66.9 us
    all_gather x1, waiting for transfers between devices, local(): tables = lax.all_gather(table, 'grp', axis=0, tiled=True)  39.1 us
    psum x1, waiting for transfers between devices, local(): all_sums, all_totals = lax.psum((sums, totals), 'row')  34.9 us
    gather x1, local copies, waits for them, and re-layouts, local(): homes = jnp.take(home_pos, block_list)  23 us
    another operation x1, loops' own time, local(): scores = lax.map(one_block, (masked, alive, mine_groups))  20 us
    dynamic_slice x32, local copies, waits for them, and re-layouts, local(): scores = lax.map(one_block, (masked, alive, mine_groups))  19.5 us
    mul x1, other arithmetic, local(): masked = row_blocks * alive_half[:, :, None]  7.24 us
  transfers between devices with their start and end apart: 4, of which 4 were waited for; matrix products, arithmetic and copies ran while one was open for 4% of the time, Pallas kernels for 0%

commit v1 on v0

v1 whole, which is shorter than its diff:
```python
import functools
import math

import jax
import jax.numpy as jnp
from jax import lax
from jax.experimental import pallas as pl
from jax.experimental.pallas import tpu as pltpu
from jax.sharding import PartitionSpec as P

PRIOR = 16
MESH = pl.DeviceIdType.MESH
LANES = 128
NT = (((1,), (1,)), ((), ()))


def iota(shape, dim):
    return lax.broadcasted_iota(jnp.int32, shape, dim)


def sums_kernel(bl, hp, cnt, keep_ref, vec_ref, vec_hbm, msg_ref, xmsg_ref, fr_ref, pick_ref,
                sums, alive, sems, *, blocks, lists_group, n_groups, n_rows):
    step = pl.program_id(0)
    steps = pl.num_programs(0)
    g = lax.axis_index("grp")
    d = lax.axis_index("row")
    base = (g * n_rows + d) * blocks

    def fetch(j):
        first = pl.multiple_of(pick_ref[4 + j] * LANES, LANES)
        return pltpu.make_async_copy(vec_hbm.at[pl.ds(first, LANES), :], fr_ref.at[j], sems.at[j])

    @pl.when(step == 0)
    def _():
        rows = iota((blocks, LANES), 0)
        limit = jnp.zeros((blocks, LANES), jnp.int32)
        picks = [jnp.int32(-1)] * (n_groups - 1)
        for k in range(blocks):
            limit = jnp.where(rows == k, cnt[k], limit)
            home = hp[bl[base + k]]
            away = lax.rem(home // lists_group - g + n_groups, n_groups)
            picks = [jnp.where(away == j + 1, k, pick) for j, pick in enumerate(picks)]
        alive[...] = jnp.where(iota((blocks, LANES), 1) < limit, keep_ref[...], 0).astype(jnp.float32)
        for j, pick in enumerate(picks):
            pick_ref[j] = pick
            pick_ref[4 + j] = jnp.maximum(pick, 0)
            fetch(j).start()

    rows8 = iota((8, LANES), 0)
    mine = alive[pl.ds(pl.multiple_of(step * 8, 8), 8), :]
    weights = jnp.concatenate(
        [jnp.where(rows8 == j, mine, 0.0).astype(jnp.bfloat16) for j in range(8)], axis=1
    )
    sums[pl.ds(pl.multiple_of(step * 8, 8), 8), :] = jnp.dot(
        weights, vec_ref[...], preferred_element_type=jnp.float32
    )

    @pl.when(step == steps - 1)
    def _():
        lane8 = iota((8, LANES), 1)
        first = lax.rem(d, 4) * blocks
        slots = jnp.zeros((8, LANES), jnp.int32)
        here = rows8 == d // 4
        for k in range(blocks):
            home = hp[bl[base + k]]
            slot = jnp.where(home // lists_group == g, lax.rem(home, lists_group) + 1, 0)
            slots = jnp.where(lane8 == first + k, slot, slots)
        counts = jnp.sum(alive[...], axis=1, keepdims=True)
        placed = jnp.where(iota((blocks, LANES), 1) == first + iota((blocks, LANES), 0), counts, 0.0)
        counts_row = jnp.sum(placed, axis=0, keepdims=True)
        code = jnp.where(here & (slots > 0), slots.astype(jnp.float32) * 256.0 + counts_row, 0.0)
        slabs = sums.shape[1] // LANES
        for s in range(slabs):
            msg_ref[s, 0:blocks, :] = sums[:, s * LANES:(s + 1) * LANES]
            msg_ref[s, blocks:blocks + 8, :] = code
        for j in range(n_groups - 1):
            pick = pick_ref[4 + j]
            valid = jnp.where(pick_ref[j] >= 0, 1.0, 0.0).astype(jnp.float32)
            row = sums[pl.ds(pick, 1), :] * valid
            count = jnp.sum(alive[pl.ds(pick, 1), :], axis=1, keepdims=True)
            slot = lax.rem(hp[bl[base + pick]], lists_group) + 1
            value = (slot.astype(jnp.float32) * 256.0 + count) * valid
            at = (rows8 == 3 + d // 16) & (lane8 == 8 * lax.rem(d, 16) + j)
            for s in range(slabs):
                xmsg_ref[j, s] = jnp.where(
                    rows8 == j, row[:, s * LANES:(s + 1) * LANES], jnp.where(at, value, 0.0)
                )
            fetch(j).wait()


def gather_kernel(msg, xmsg, fr, old, table_out, norms_out, fs_out,
                  g1, a1, xin, arr, g2, a2, frin, tab,
                  s1s, s1r, s1b_s, s1b_r, xs, xr, fs_s, fs_r, s2s, s2r, s2b_s, s2b_r,
                  s3s, s3r, rs, rr, ls, *, blocks, n_groups, factor):
    g = lax.axis_index("grp")
    d = lax.axis_index("row")
    core = lax.rem(d, 2)
    y = lax.rem(d // 2, 4)
    z = d // 8
    flat = core == 0
    u = jnp.where(flat, y, z)
    v = jnp.where(flat, z, y)
    sid = core * 4 + u
    partner = d + 1 - 2 * core

    def row_of(zz, yy, cc):
        return (zz * 4 + yy) * 2 + cc

    def along_u(i):
        w = lax.rem(u + i, 4)
        return jnp.where(flat, row_of(z, w, core), row_of(w, y, core))

    def along_v(i):
        w = lax.rem(v + i, 4)
        return jnp.where(flat, row_of(w, y, core), row_of(z, w, core))

    def copy(src, dst, send, recv, where):
        return pltpu.make_async_remote_copy(
            src_ref=src, dst_ref=dst, send_sem=send, recv_sem=recv,
            device_id=where, device_id_type=MESH,
        )

    barrier = pltpu.get_barrier_semaphore()
    greeted = 0
    for i in range(1, 4):
        for c in range(2):
            pl.semaphore_signal(barrier, inc=1, device_id={"row": row_of(z, lax.rem(y + i, 4), c)},
                                device_id_type=MESH)
            pl.semaphore_signal(barrier, inc=1, device_id={"row": row_of(lax.rem(z + i, 4), y, c)},
                                device_id_type=MESH)
            greeted += 2
        pl.semaphore_signal(barrier, inc=1, device_id={"grp": lax.rem(g + i, n_groups)},
                            device_id_type=MESH)
        greeted += 1
    pl.semaphore_signal(barrier, inc=1, device_id={"row": partner}, device_id_type=MESH)
    pl.semaphore_wait(barrier, greeted + 1)

    xcopies = []
    for i in range(1, n_groups):
        where = {"grp": lax.rem(g + i, n_groups)}
        xcopies.append(copy(xmsg.at[i - 1], xin.at[i - 1], xs.at[i - 1], xr.at[i - 1], where))
        xcopies[-1].start()

    def slab_sends(src, dst, send, recv):
        out = []
        for i in range(1, 4):
            yy = lax.rem(y + i, 4)
            q = y * 2 + core
            out.append(copy(src.at[yy], dst.at[q], send.at[2 * i], recv.at[q],
                            {"row": row_of(z, yy, 0)}))
            zz = lax.rem(z + i, 4)
            q = z * 2 + core
            out.append(copy(src.at[4 + zz], dst.at[q], send.at[2 * i + 1], recv.at[q],
                            {"row": row_of(zz, y, 1)}))
        theirs = jnp.where(flat, 4 + z, y)
        q = jnp.where(flat, z, y) * 2 + core
        out.append(copy(src.at[theirs], dst.at[q], send.at[1], recv.at[q], {"row": partner}))
        for item in out:
            item.start()
        own = u * 2 + core
        local = pltpu.make_async_copy(src.at[sid], dst.at[own], recv.at[own])
        local.start()
        return out, local

    def slab_waits(started, src, dst, send, recv):
        out, local = started
        local.wait()
        own = u * 2 + core
        for i in range(1, 8):
            q = lax.rem(own + i, 8)
            copy(src.at[0], dst.at[q], send.at[0], recv.at[q], {"row": partner}).wait_recv()
        for item in out:
            item.wait_send()

    first = slab_sends(msg, g1, s1s, s1r)

    fcopies = []
    for i in range(1, n_groups):
        where = {"grp": lax.rem(g + i, n_groups)}
        fcopies.append(copy(fr.at[i - 1], frin.at[i - 1], fs_s.at[i - 1], fs_r.at[i - 1], where))

    for item in xcopies:
        item.wait()
    for item in fcopies:
        item.start()
    for s in range(8):
        arr[s] = xin[0, s] + xin[1, s] + xin[2, s]
    slab_waits(first, msg, g1, s1s, s1r)

    def plane_sends(src, dst, send, recv):
        out = []
        for i in range(1, 4):
            out.append(copy(src, dst.at[v], send.at[i], recv.at[i], {"row": along_v(i)}))
            out[-1].start()
        local = pltpu.make_async_copy(src, dst.at[v], recv.at[0])
        local.start()
        return out, local

    def plane_waits(started):
        out, local = started
        local.wait()
        for item in out:
            item.wait()

    plane = plane_sends(g1, g2, s2s, s2r)
    second = slab_sends(arr, a1, s1b_s, s1b_r)
    slab_waits(second, arr, a1, s1b_s, s1b_r)
    plane_b = plane_sends(a1, a2, s2b_s, s2b_r)
    plane_waits(plane)

    lists = tab.shape[0]
    codes = jnp.zeros((8, LANES), jnp.float32)
    for i in range(4):
        for q in range(8):
            codes = codes + g2[i, q, blocks:blocks + 8, :]
    codes = codes.astype(jnp.int32)
    target = iota((lists, LANES), 0)

    def piece(ref, zz, yy, count):
        one = jnp.where(flat, zz, yy)
        two = jnp.where(flat, yy, zz) * 2
        return [ref[one, two, 0:count, :], ref[one, two + 1, 0:count, :]]

    def split(values):
        high = values.astype(jnp.bfloat16)
        low = (values - high.astype(jnp.float32)).astype(jnp.bfloat16)
        return jnp.concatenate([high, low], axis=1)

    def chunk(rows, values):
        slots = [(row >> 8) - 1 for row in rows]
        held = [(row & 255).astype(jnp.float32) for row in rows]
        hot = jnp.concatenate(
            [jnp.where(target == slot, 1.0, 0.0).astype(jnp.bfloat16) for slot in slots], axis=1
        )
        part = jnp.dot(hot, split(values), preferred_element_type=jnp.float32)
        held = jnp.concatenate(held, axis=1)
        held = jnp.broadcast_to(held, (LANES, held.shape[1])).astype(jnp.bfloat16)
        total = lax.dot_general(hot, held, NT, preferred_element_type=jnp.float32)
        return part[:, :LANES] + part[:, LANES:], total

    sums = jnp.zeros((lists, LANES), jnp.float32)
    totals = jnp.zeros((lists, LANES), jnp.float32)
    for zz in range(4):
        values = jnp.concatenate(sum([piece(g2, zz, yy, blocks) for yy in range(4)], []), axis=0)
        part, total = chunk([codes[2 * zz:2 * zz + 1], codes[2 * zz + 1:2 * zz + 2]], values)
        sums, totals = sums + part, totals + total
    plane_waits(plane_b)
    codes = jnp.zeros((8, LANES), jnp.float32)
    for i in range(4):
        for q in range(8):
            codes = codes + a2[i, q]
    codes = codes[3:5].astype(jnp.int32)
    values = jnp.concatenate(
        sum([piece(a2, zz, yy, 8) for zz in range(4) for yy in range(4)], []), axis=0
    )
    part, total = chunk([codes[0:1], codes[1:2]], values)
    sums, totals = sums + part, totals + total

    def columns(s):
        return pl.ds(pl.multiple_of(s * LANES, LANES), LANES)

    previous = old[:, columns(sid)].astype(jnp.float32)
    prior = 1.0 * PRIOR
    tab[:, columns(sid)] = ((sums + prior * previous) / (totals + prior)).astype(jnp.bfloat16)

    spread = []
    for i in range(1, 4):
        ref = tab.at[:, columns(sid)]
        spread.append(copy(ref, ref, s3s.at[i], s3r.at[i], {"row": along_u(i)}))
        spread[-1].start()
    ref = tab.at[:, columns(sid)]
    relays = [copy(ref, ref, rs.at[0], rr.at[0], {"row": partner})]
    relays[0].start()
    for i in range(1, 4):
        ref = tab.at[:, columns(core * 4 + lax.rem(u - i + 4, 4))]
        copy(ref, ref, s3s.at[i], s3r.at[i], {"row": partner}).wait_recv()
        relays.append(copy(ref, ref, rs.at[i], rr.at[i], {"row": partner}))
        relays[-1].start()
    for i in range(4):
        w = jnp.where(flat, z, y)
        ref = tab.at[:, columns((1 - core) * 4 + lax.rem(w - i + 4, 4))]
        copy(ref, ref, rs.at[i], rr.at[i], {"row": partner}).wait_recv()
    out = pltpu.make_async_copy(tab, table_out, ls.at[0])
    out.start()

    ones = jnp.ones((8, tab.shape[1]), jnp.bfloat16)
    squares = jnp.square(tab[...].astype(jnp.float32))
    high = squares.astype(jnp.bfloat16)
    low = (squares - high.astype(jnp.float32)).astype(jnp.bfloat16)
    norms = lax.dot_general(ones, high, NT, preferred_element_type=jnp.float32)
    norms = norms + lax.dot_general(ones, low, NT, preferred_element_type=jnp.float32)
    norms_out[...] = norms
    for item in fcopies:
        item.wait()
    for j in range(n_groups - 1):
        dots = lax.dot_general(frin[j], tab[...], NT, preferred_element_type=jnp.float32)
        fs_out[j] = ((2.0 * dots - norms[0:1]) * factor).astype(jnp.bfloat16)
    for item in spread:
        item.wait_send()
    for item in relays:
        item.wait_send()
    out.wait()


def alive_column(row):
    eye = iota((LANES, LANES), 0) == iota((LANES, LANES), 1)
    return jnp.sum(jnp.where(eye, row, 0.0), axis=1, keepdims=True)


def scores_kernel(cnt, keep_ref, vec_ref, table, norms, scores_ref, new_ref, *, factor, share):
    step = pl.program_id(0)
    d = lax.axis_index("row")

    @pl.when(step == 0)
    def _():
        new_ref[...] = table[pl.ds(pl.multiple_of(d * share, share), share), :]

    n = vec_ref.shape[0] // LANES
    lane = iota((1, LANES), 1)
    dots = lax.dot_general(vec_ref[...], table[...], NT, preferred_element_type=jnp.float32)
    for b in range(n):
        k = step * n + b
        row = jnp.where(lane < cnt[k], keep_ref[pl.ds(k, 1), :], 0).astype(jnp.float32)
        scores_ref[b * LANES:(b + 1) * LANES, :] = (
            (2.0 * dots[b * LANES:(b + 1) * LANES] - norms[0:1]) * factor
        ) * alive_column(row)


def merge_kernel(pick, cnt, keep_ref, b0, b1, b2, _, scores_ref, held, sems):
    lane = iota((1, LANES), 1)
    backs = (b0, b1, b2)

    def put(j):
        first = pl.multiple_of(pick[4 + j] * LANES, LANES)
        return pltpu.make_async_copy(held.at[j], scores_ref.at[pl.ds(first, LANES), :], sems.at[j])

    for j, back in enumerate(backs):
        @pl.when(pick[j] >= 0)
        def _():
            k = pick[4 + j]
            row = jnp.where(lane < cnt[k], keep_ref[pl.ds(k, 1), :], 0).astype(jnp.float32)
            held[j] = back[...].astype(jnp.float32) * alive_column(row)
            put(j).start()
    for j in range(len(backs)):
        @pl.when(pick[j] >= 0)
        def _():
            put(j).wait()


def local(vectors, keep_bits, counts, block_list, home_pos, old_centroids):
    n_groups = lax.axis_size("grp")
    n_rows = lax.axis_size("row")
    blocks = counts.shape[0]
    total_rows, width = vectors.shape
    block_rows = total_rows // blocks
    lists_group = old_centroids.shape[0]
    factor = 1.0 / math.sqrt(width)
    slabs = width // LANES
    away = n_groups - 1
    keep = keep_bits.reshape(blocks, block_rows)
    whole = pl.BlockSpec(memory_space=pltpu.VMEM)
    f32, bf16 = jnp.float32, jnp.bfloat16

    def full(*shape):
        return pl.BlockSpec(shape, lambda *_: (0,) * len(shape))

    rows = 8 * block_rows
    msg, xmsg, leaving, picks = pl.pallas_call(
        functools.partial(sums_kernel, blocks=blocks, lists_group=lists_group,
                          n_groups=n_groups, n_rows=n_rows),
        out_shape=(
            jax.ShapeDtypeStruct((slabs, blocks + 8, LANES), f32),
            jax.ShapeDtypeStruct((away, slabs, 8, LANES), f32),
            jax.ShapeDtypeStruct((away, block_rows, width), bf16),
            jax.ShapeDtypeStruct((8,), jnp.int32),
        ),
        grid_spec=pltpu.PrefetchScalarGridSpec(
            num_scalar_prefetch=3,
            grid=(total_rows // rows,),
            in_specs=[
                full(blocks, block_rows),
                pl.BlockSpec((rows, width), lambda i, *_: (i, 0)),
                pl.BlockSpec(memory_space=pl.ANY),
            ],
            out_specs=(
                full(slabs, blocks + 8, LANES),
                full(away, slabs, 8, LANES),
                full(away, block_rows, width),
                pl.BlockSpec(memory_space=pltpu.SMEM),
            ),
            scratch_shapes=[
                pltpu.VMEM((blocks, width), f32),
                pltpu.VMEM((blocks, LANES), f32),
                pltpu.SemaphoreType.DMA((away,)),
            ],
        ),
        name="block_sums",
    )(block_list, home_pos, counts, keep, vectors, vectors)

    dma = pltpu.SemaphoreType.DMA
    table, norms, found = pl.pallas_call(
        functools.partial(gather_kernel, blocks=blocks, n_groups=n_groups, factor=factor),
        out_shape=(
            jax.ShapeDtypeStruct((lists_group, width), bf16),
            jax.ShapeDtypeStruct((8, lists_group), f32),
            jax.ShapeDtypeStruct((away, block_rows, lists_group), bf16),
        ),
        in_specs=[whole] * 4,
        out_specs=(pl.BlockSpec(memory_space=pl.ANY), whole, whole),
        scratch_shapes=[
            pltpu.VMEM((8, blocks + 8, LANES), f32),
            pltpu.VMEM((8, 8, LANES), f32),
            pltpu.VMEM((away, slabs, 8, LANES), f32),
            pltpu.VMEM((slabs, 8, LANES), f32),
            pltpu.VMEM((4, 8, blocks + 8, LANES), f32),
            pltpu.VMEM((4, 8, 8, LANES), f32),
            pltpu.VMEM((away, block_rows, width), bf16),
            pltpu.VMEM((lists_group, width), bf16),
            dma((8,)), dma((8,)), dma((8,)), dma((8,)),
            dma((4,)), dma((4,)), dma((4,)), dma((4,)),
            dma((4,)), dma((4,)), dma((4,)), dma((4,)),
            dma((4,)), dma((4,)), dma((4,)), dma((4,)),
            dma((1,)),
        ],
        compiler_params=pltpu.CompilerParams(collective_id=0, has_side_effects=True),
        name="table_exchange",
    )(msg, xmsg, leaving, old_centroids)

    backs = [
        lax.ppermute(found[j], "grp", [(s, (s - j - 1) % n_groups) for s in range(n_groups)])
        for j in range(away)
    ]

    rows = 4 * block_rows
    scores, new_centroids = pl.pallas_call(
        functools.partial(scores_kernel, factor=factor, share=lists_group // n_rows),
        out_shape=(
            jax.ShapeDtypeStruct((total_rows, lists_group), f32),
            jax.ShapeDtypeStruct((lists_group // n_rows, width), bf16),
        ),
        grid_spec=pltpu.PrefetchScalarGridSpec(
            num_scalar_prefetch=1,
            grid=(total_rows // rows,),
            in_specs=[
                full(blocks, block_rows),
                pl.BlockSpec((rows, width), lambda i, *_: (i, 0)),
                full(lists_group, width),
                full(8, lists_group),
            ],
            out_specs=(
                pl.BlockSpec((rows, lists_group), lambda i, *_: (i, 0)),
                full(lists_group // n_rows, width),
            ),
        ),
        cost_estimate=pl.CostEstimate(
            flops=2 * total_rows * width * lists_group,
            bytes_accessed=total_rows * (2 * width + 4 * lists_group),
            transcendentals=0,
        ),
        name="scores",
    )(counts, keep, vectors, table, norms)

    scores = pl.pallas_call(
        merge_kernel,
        out_shape=jax.ShapeDtypeStruct(scores.shape, f32),
        grid_spec=pltpu.PrefetchScalarGridSpec(
            num_scalar_prefetch=2,
            grid=(1,),
            in_specs=[full(blocks, block_rows)] + [full(block_rows, lists_group)] * away
            + [pl.BlockSpec(memory_space=pl.ANY)],
            out_specs=pl.BlockSpec(memory_space=pl.ANY),
            scratch_shapes=[
                pltpu.VMEM((away, block_rows, lists_group), f32),
                pltpu.SemaphoreType.DMA((away,)),
            ],
        ),
        input_output_aliases={6: 0},
        name="merge",
    )(picks, counts, keep, *backs, scores)
    return new_centroids, scores


def solution(mesh):
    in_specs = (
        P(("grp", "row"), None),
        P(("grp", "row")),
        P(("grp", "row")),
        P(),
        P(),
        P("grp", None),
    )
    out_specs = (P(("grp", "row"), None), P(("grp", "row"), None))
    return jax.shard_map(local, mesh=mesh, in_specs=in_specs, out_specs=out_specs, check_vma=False)
```

time: 345 us -> 63.2 us (0.18)
  matrix products: 88.5 us -> 0 us
  waiting for transfers between devices: 79.4 us -> 0.01 us
  blocking collectives: 66.9 us -> 0 us
  Pallas kernels: 0 us -> 56.8 us
  local copies, waits for them, and re-layouts: 49.8 us -> 1.75 us
  loops' own time: 20 us -> 0 us
  other arithmetic: 16.7 us -> 0 us
  between operations: 14.2 us -> 0.7 us
  starting transfers between devices: 8.1 us -> 3.46 us
    dot_general x37 -> x0, matrix products: 88.5 us -> none  [the longest x32 80.2 us: score_rows(): lax.dot_general(rows, table, (((1,), (1,)), ((), ())), preferred_element_...]
    psum x1 -> x0, blocking collectives: 66.9 us -> none  [local(): all_sums, all_totals = lax.psum((sums, totals), 'row')]
    pallas_call x0 -> x4, Pallas kernels: none -> 56.8 us  [the longest x1 34.9 us: local(): pl.pallas_call(functools.partial(gather_kernel, blocks=blocks, n_groups=n...]
    all_gather x1 -> x0, waiting for transfers between devices: 39.1 us -> none  [local(): tables = lax.all_gather(table, 'grp', axis=0, tiled=True)]
    psum x1 -> x0, waiting for transfers between devices: 34.9 us -> none  [local(): all_sums, all_totals = lax.psum((sums, totals), 'row')]
    gather x4 -> x0, local copies, waits for them, and re-layouts: 24.9 us -> none  [the longest x1 23 us: local(): homes = jnp.take(home_pos, block_list)]
    dynamic_slice x66 -> x0, local copies, waits for them, and re-layouts: 23.5 us -> none  [the longest x32 19.5 us: local(): scores = lax.map(one_block, (masked, alive, mine_groups))]
    another operation x1 -> x0, loops' own time: 20 us -> none  [local(): scores = lax.map(one_block, (masked, alive, mine_groups))]
  transfers between devices with their start and end apart: 4 -> 3, of which waited for: 4 -> 0; matrix products, arithmetic and copies ran while one was open for 4% -> 0% of each run, Pallas kernels for 0% -> 19%
where the time goes in v1:
time: 63.2 us; the launch traced here: 62.7 us
  Pallas kernels  56.8 us (90%)
  starting transfers between devices  3.46 us (5%)
  local copies, waits for them, and re-layouts  1.75 us (3%)
  between operations  0.7 us (1%)
    pallas_call x1, Pallas kernels, local(): pl.pallas_call(functools.partial(gather_kernel, blocks=blocks, n_groups=n...  34.9 us
    pallas_call x1, Pallas kernels, local(): pl.pallas_call(functools.partial(scores_kernel, factor=factor, share=list...  12 us
    pallas_call x1, Pallas kernels, local(): pl.pallas_call(functools.partial(sums_kernel, blocks=blocks, lists_group=...  7.35 us
    ppermute x3, starting transfers between devices, local(): lax.ppermute(found[j], 'grp', [(s, (s - j - 1) % n_groups) for s in range...  3.46 us
    pallas_call x1, Pallas kernels, local(): pl.pallas_call(merge_kernel, out_shape=jax.ShapeDtypeStruct(scores.shape,...  2.55 us
  transfers between devices with their start and end apart: 3, of which 0 were waited for; matrix products, arithmetic and copies ran while one was open for 0% of the time, Pallas kernels for 19%

profile of v1, /device:TPU:1, one launch (start us, length us, event | category | flops | bytes accessed | tf_op | source)
XLA Modules:
  0.0 62.7 jit_solution(775853378302640698)
XLA Ops:
  0.6 7.3 %block_sums.1 = (f32[8,40,128]{2,1,0:T(8,128)}, f32[3,8,8,128]{3,2,1,0:T(8,128)}, bf16[3,128,1024]{2,1,0:T(8,128)(2,1)}, s32[8]{0:T(128)}) custom-call(s32[4096]{0:T(1024)} %bl.1, s32[2048]{0:T(1024)} %hp.1, s32[32]{0:T(128)} %cnt.5, s32[32,128]{1,0:T(8,128)} %bitcast.7, bf16[4096,1024]{1,0:T(8,128)(2,1)} %vec_ref.3, bf16[4096,1024]{1,0:T(8,128)(2,1)} %vec_ref.3), custom_call_target="tpu_custom_call" | custom-call | tf_op jit(solution)/shard_map/block_sums/pallas_call | solution.py:368
  8.0 34.9 %table_exchange.1 = (bf16[512,1024]{1,0:T(8,128)(2,1)}, f32[8,512]{1,0:T(8,128)}, bf16[3,128,512]{2,1,0:T(8,128)(2,1)}) custom-call(f32[8,40,128]{2,1,0:T(8,128)} %get-tuple-element.11.msg, f32[3,8,8,128]{3,2,1,0:T(8,128)} %get-tuple-element.12.xmsg, bf16[3,128,1024]{2,1,0:T(8,128)(2,1)} %get-tuple-element.13.fr, bf16[512,1024]{1,0:T(8,128)(2,1)} %old.1), custom_call_target="tpu_custom_call" | custom-call | tf_op jit(solution)/shard_map/table_exchange/pallas_call | solution.py:401
  42.9 1.1 %slice_bitcast_fusion = (bf16[128,512]{1,0:T(8,128)(2,1)S(1)}, bf16[128,512]{1,0:T(8,128)(2,1)S(1)}, bf16[128,512]{1,0:T(8,128)(2,1)S(1)}) fusion(bf16[3,128,512]{2,1,0:T(8,128)(2,1)} %get-tuple-element.18), kind=kLoop, calls=%fused_computation | loop fusion | bytes 786432 | tf_op jit(solution)/shard_map/squeeze | solution.py:430
  43.9 0.1 collective-permute-start.2
  44.0 2.2 %collective-permute-start.1 = (bf16[128,512]{1,0:T(8,128)(2,1)S(1)}, bf16[128,512]{1,0:T(8,128)(2,1)S(1)}, u32[]{:S(2)}, u32[]{:S(2)}) collective-permute-start(bf16[128,512]{1,0:T(8,128)(2,1)S(1)} %get-tuple-element.21), channel_id=1, source_target_pairs={{0,64},{32,96},{64,0},{96,32},{1,65},{33,97},{65,1},{97,33},{2,66}... | collective-permute-start | bytes 393224 | tf_op jit(solution)/shard_map/ppermute | solution.py:430
  46.2 1.1 %collective-permute-start = (bf16[128,512]{1,0:T(8,128)(2,1)S(1)}, bf16[128,512]{1,0:T(8,128)(2,1)S(1)}, u32[]{:S(2)}, u32[]{:S(2)}) collective-permute-start(bf16[128,512]{1,0:T(8,128)(2,1)S(1)} %get-tuple-element.22), channel_id=1, source_target_pairs={{0,96},{32,0},{64,32},{96,64},{1,97},{33,1},{65,33},{97,65},{2,98}... | collective-permute-start | bytes 393224 | tf_op jit(solution)/shard_map/ppermute | solution.py:430
  47.4 12.0 %scores.1 = (f32[4096,512]{1,0:T(8,128)}, bf16[16,1024]{1,0:T(8,128)(2,1)}) custom-call(s32[32]{0:T(128)} %cnt.5, s32[32,128]{1,0:T(8,128)} %bitcast.8, bf16[4096,1024]{1,0:T(8,128)(2,1)} %vec_ref.3, bf16[512,1024]{1,0:T(8,128)(2,1)} %get-tuple-element.14.table, f32[8,512]{1,0:T(8,128)} %get-tuple-element.15.norms), custom_call_target="tpu_custom_call" | custom-call | flops 4294967296 | bytes 16777216 | tf_op jit(solution)/shard_map/scores/pallas_call | solution.py:435
  59.4 0.0 collective-permute-done.2.b2
  59.4 0.0 copy-start
  59.4 0.0 collective-permute-done.1.b1
  59.4 0.0 copy-start.1
  59.5 0.0 collective-permute-done.b0
  59.5 0.0 copy-start.2
  59.5 0.6 copy-done
  60.1 0.1 copy-done.1
  60.1 0.0 copy-done.2
  60.2 2.5 %merge.1 = f32[4096,512]{1,0:T(8,128)} custom-call(s32[8]{0:T(128)} %get-tuple-element.17.pick, s32[32]{0:T(128)} %cnt.5, s32[32,128]{1,0:T(8,128)} %bitcast.9, bf16[128,512]{1,0:T(8,128)(2,1)} %copy-done.2, bf16[128,512]{1,0:T(8,128)(2,1)} %copy-done.1, bf16[128,512]{1,0:T(8,128)(2,1)} %copy-done, ...), custom_call_target="tpu_custom_call", output_to_operand_aliasing={{}: (6, {})} | custom-call | tf_op jit(solution)/shard_map/merge/pallas_call | solution.py:463
Async XLA Ops:
  43.9 15.5 %collective-permute-start.2 = (bf16[128,512]{1,0:T(8,128)(2,1)S(1)}, bf16[128,512]{1,0:T(8,128)(2,1)S(1)}, u32[]{:S(2)}, u32[]{:S(2)}) collective-permute-start(bf16[128,512]{1,0:T(8,128)(2,1)S(1)} %get-tuple-element.20), channel_id=1, source_target_pairs={{0,32},{32,64},{64,96},{96,0},{1,33},{33,65},{65,97},{97,1},{2,34}... | collective-permute-start | bytes 393224 | tf_op jit(solution)/shard_map/ppermute | solution.py:430
  44.0 15.4 %collective-permute-start.1 = (bf16[128,512]{1,0:T(8,128)(2,1)S(1)}, bf16[128,512]{1,0:T(8,128)(2,1)S(1)}, u32[]{:S(2)}, u32[]{:S(2)}) collective-permute-start(bf16[128,512]{1,0:T(8,128)(2,1)S(1)} %get-tuple-element.21), channel_id=1, source_target_pairs={{0,64},{32,96},{64,0},{96,32},{1,65},{33,97},{65,1},{97,33},{2,66}... | collective-permute-start | bytes 393224 | tf_op jit(solution)/shard_map/ppermute | solution.py:430
  46.2 13.2 %collective-permute-start = (bf16[128,512]{1,0:T(8,128)(2,1)S(1)}, bf16[128,512]{1,0:T(8,128)(2,1)S(1)}, u32[]{:S(2)}, u32[]{:S(2)}) collective-permute-start(bf16[128,512]{1,0:T(8,128)(2,1)S(1)} %get-tuple-element.22), channel_id=1, source_target_pairs={{0,96},{32,0},{64,32},{96,64},{1,97},{33,1},{65,33},{97,65},{2,98}... | collective-permute-start | bytes 393224 | tf_op jit(solution)/shard_map/ppermute | solution.py:430
  59.4 0.6 %copy-start = (bf16[128,512]{1,0:T(8,128)(2,1)}, bf16[128,512]{1,0:T(8,128)(2,1)S(1)}, u32[]{:S(2)}) copy-start(bf16[128,512]{1,0:T(8,128)(2,1)S(1)} %collective-permute-done.2.b2) | copy-start | bytes 393220
  59.4 0.7 %copy-start.1 = (bf16[128,512]{1,0:T(8,128)(2,1)}, bf16[128,512]{1,0:T(8,128)(2,1)S(1)}, u32[]{:S(2)}) copy-start(bf16[128,512]{1,0:T(8,128)(2,1)S(1)} %collective-permute-done.1.b1) | copy-start | bytes 393220
  59.5 0.7 %copy-start.2 = (bf16[128,512]{1,0:T(8,128)(2,1)}, bf16[128,512]{1,0:T(8,128)(2,1)S(1)}, u32[]{:S(2)}) copy-start(bf16[128,512]{1,0:T(8,128)(2,1)S(1)} %collective-permute-done.b0) | copy-start | bytes 393220

commit v2 on v0

v2 whole, which is shorter than its diff:
```python
import functools
import math

import jax
import jax.numpy as jnp
from jax import lax
from jax.experimental import pallas as pl
from jax.experimental.pallas import tpu as pltpu
from jax.sharding import PartitionSpec as P

PRIOR = 16
MESH = pl.DeviceIdType.MESH
LANES = 128
NT = (((1,), (1,)), ((), ()))


def iota(shape, dim):
    return lax.broadcasted_iota(jnp.int32, shape, dim)


def table_kernel(bl_hbm, hp_hbm, cnt_hbm, keep_hbm, vec_hbm, old_hbm,
                 vec, table, norms_out, f0, f1, f2,
                 bl, hp, cnt, keep, alive, sums, msg, xmsg, leaving, previous,
                 xin, arr, g2, a2, passing, arrived,
                 load_sem, small_sem, p1_s, p1_r, p1b_s, p1b_r, x_s, x_r, bulk_s, bulk_r,
                 p2_s, p2_r, p2b_s, p2b_r, p3_s, p3_r, mate_s, mate_r,
                 *, n_groups, n_rows, factor):
    blocks = alive.shape[0]
    slabs = msg.shape[0]
    g = lax.axis_index("grp")
    d = lax.axis_index("row")
    core = lax.rem(d, 2)
    y = lax.rem(d // 2, 4)
    z = d // 8
    flat = core == 0
    u = jnp.where(flat, y, z)
    v = jnp.where(flat, z, y)
    sid = core * 4 + u
    partner = d + 1 - 2 * core
    mate = {"row": partner}
    base = (g * n_rows + d) * blocks
    rows8 = iota((8, LANES), 0)
    lane8 = iota((8, LANES), 1)

    def row_of(zz, yy, cc):
        return (zz * 4 + yy) * 2 + cc

    def along_u(i):
        w = lax.rem(u + i, 4)
        return {"row": jnp.where(flat, row_of(z, w, core), row_of(w, y, core))}

    def along_v(i):
        w = lax.rem(v + i, 4)
        return {"row": jnp.where(flat, row_of(w, y, core), row_of(z, w, core))}

    def group(i):
        return {"grp": lax.rem(g + i, n_groups)}

    def copy(src, dst, send, recv, where):
        return pltpu.make_async_remote_copy(
            src_ref=src, dst_ref=dst, send_sem=send, recv_sem=recv,
            device_id=where, device_id_type=MESH,
        )

    def columns(s):
        return pl.ds(pl.multiple_of(s * LANES, LANES), LANES)

    small = [
        pltpu.make_async_copy(src, dst, small_sem.at[i])
        for i, (src, dst) in enumerate(((bl_hbm, bl), (hp_hbm, hp), (cnt_hbm, cnt), (keep_hbm, keep)))
    ]
    for item in small:
        item.start()
    chunks = load_sem.shape[0]
    size = vec.shape[0] // chunks
    loads = [
        pltpu.make_async_copy(
            vec_hbm.at[pl.ds(i * size, size), :], vec.at[pl.ds(i * size, size), :], load_sem.at[i]
        )
        for i in range(chunks)
    ]
    for item in loads:
        item.start()
    prior_load = pltpu.make_async_copy(old_hbm.at[:, columns(sid)], previous, small_sem.at[4])
    prior_load.start()

    barrier = pltpu.get_barrier_semaphore()
    peers = [mate]
    for i in range(1, 4):
        for c in range(2):
            peers.append({"row": row_of(z, lax.rem(y + i, 4), c)})
            peers.append({"row": row_of(lax.rem(z + i, 4), y, c)})
    for i in range(1, n_groups):
        peers.append(group(i))
    for where in peers:
        pl.semaphore_signal(barrier, inc=1, device_id=where, device_id_type=MESH)

    for item in small:
        item.wait()
    rows = iota((blocks, LANES), 0)
    lanes = iota((blocks, LANES), 1)
    lane = iota((1, LANES), 1)
    eye = iota((blocks, blocks), 0) == iota((blocks, blocks), 1)
    limit = jnp.sum(jnp.where(eye, cnt[...], 0), axis=1, keepdims=True)
    alive[...] = jnp.where(lanes < limit, keep[...], 0).astype(jnp.float32)
    first = lax.rem(d, 4) * blocks
    counts = jnp.sum(alive[...], axis=1, keepdims=True)
    counts_row = jnp.sum(jnp.where(lanes == first + rows, counts, 0.0), axis=0, keepdims=True)

    lists = table.shape[0]
    per_group = lists // LANES
    homes = jnp.concatenate([hp[pl.ds(g * per_group + i, 1), :] for i in range(per_group)], axis=1)
    line = iota((8, lists), 0)
    digits = jnp.where(line == 0, homes >> 8, jnp.where(line == 1, homes & 255, 0))
    listed = bl[pl.ds(g * (n_rows * blocks // LANES) + d // 4, 1), :] - g * lists
    hot = jnp.where(iota((lists, LANES), 0) == listed, 1.0, 0.0).astype(jnp.bfloat16)
    found = jnp.dot(
        digits.astype(jnp.float32).astype(jnp.bfloat16), hot, preferred_element_type=jnp.float32
    ).astype(jnp.int32)
    home = found[0:1] * 256 + found[1:2]
    slot = lax.rem(home, lists)
    away = lax.rem(home // lists - g + n_groups, n_groups)
    own_lanes = (lane >= first) & (lane < first + blocks)
    worth = (slot + 1).astype(jnp.float32) * 256.0 + counts_row
    staying = jnp.where(own_lanes & (away == 0), worth, 0.0)
    code = jnp.where(rows8 == d // 4, staying, 0.0)
    for s in range(slabs):
        msg[s, blocks:blocks + 8, :] = code
    values, marks = [], []
    for j in range(n_groups - 1):
        going = jnp.where(own_lanes & (away == j + 1), 1.0, 0.0)
        values.append(jnp.sum(going * worth, axis=1, keepdims=True))
        marks.append(jnp.sum(jnp.where(lanes == first + rows, going, 0.0), axis=1, keepdims=True))

    def keep_leaving(i):
        for j, mark in enumerate(marks):
            part = jnp.zeros((LANES, vec.shape[1]), jnp.bfloat16)
            for k in range(i * 8, i * 8 + 8):
                weight = mark[k:k + 1].astype(jnp.bfloat16)
                part = part + vec[k * LANES:(k + 1) * LANES, :] * weight
            leaving[j] = part if i == 0 else leaving[j] + part

    per = chunks * 8 // blocks
    for i in range(blocks // 8):
        for item in loads[i * per:(i + 1) * per]:
            item.wait()
        mine = alive[i * 8:(i + 1) * 8, :]
        weights = jnp.concatenate(
            [jnp.where(rows8 == j, mine, 0.0).astype(jnp.bfloat16) for j in range(8)], axis=1
        )
        part = jnp.dot(
            weights, vec[i * 8 * LANES:(i + 1) * 8 * LANES, :], preferred_element_type=jnp.float32
        )
        sums[i * 8:(i + 1) * 8, :] = part
        for s in range(slabs):
            msg[s, i * 8:(i + 1) * 8, :] = part[:, s * LANES:(s + 1) * LANES]
        if i < blocks // 8 - 1:
            keep_leaving(i)

    pl.semaphore_wait(barrier, len(peers))

    def slab_sends(src, dst, send, recv):
        out = []
        for i in range(1, 4):
            yy = lax.rem(y + i, 4)
            q = y * 2 + core
            out.append(copy(src.at[yy], dst.at[z, q], send.at[2 * i], recv.at[q],
                            {"row": row_of(z, yy, 0)}))
            zz = lax.rem(z + i, 4)
            q = z * 2 + core
            out.append(copy(src.at[4 + zz], dst.at[y, q], send.at[2 * i + 1], recv.at[q],
                            {"row": row_of(zz, y, 1)}))
        theirs = jnp.where(flat, 4 + z, y)
        q = jnp.where(flat, z, y) * 2 + core
        out.append(copy(src.at[theirs], dst.at[jnp.where(flat, y, z), q], send.at[1], recv.at[q], mate))
        for item in out:
            item.start()
        own = u * 2 + core
        kept = pltpu.make_async_copy(src.at[sid], dst.at[v, own], recv.at[own])
        kept.start()
        return out, kept

    def slab_waits(started, src, dst, send, recv):
        out, kept = started
        kept.wait()
        own = u * 2 + core
        for i in range(1, 8):
            q = lax.rem(own + i, 8)
            copy(src.at[0], dst.at[v, q], send.at[0], recv.at[q], mate).wait_recv()
        for item in out:
            item.wait_send()

    def ring_start(near, at, part, send, recv):
        right, left = near(1), near(3)
        out = [
            copy(part(at, h), part(at, h), send.at[n], recv.at[n], to)
            for n, (h, to) in enumerate(((0, right), (1, left), (1, right), (0, left)))
        ]
        for item in out:
            item.start()
        return out

    def ring_wait(near, at, part, send, recv, n):
        frm = (3, 1, 3, 1, 2, 2)[n]
        ref = part(lax.rem(at + frm, 4), (0, 1, 1, 0, 0, 1)[n])
        copy(ref, ref, send.at[n], recv.at[n], near(1)).wait_recv()

    def ring_relay(near, at, part, send, recv):
        out = []
        for n, (frm, h, to) in enumerate(((3, 0, 1), (1, 1, 3))):
            ring_wait(near, at, part, send, recv, n)
            ref = part(lax.rem(at + frm, 4), h)
            out.append(copy(ref, ref, send.at[4 + n], recv.at[4 + n], near(to)))
            out[-1].start()
        return out

    first_sent = slab_sends(msg, g2, p1_s, p1_r)
    for j in range(n_groups - 1):
        row = jnp.sum(sums[...] * marks[j], axis=0, keepdims=True)
        at = (rows8 == 3 + d // 16) & (lane8 == 8 * lax.rem(d, 16) + j)
        for s in range(slabs):
            xmsg[j, s] = jnp.where(
                rows8 == j, row[:, s * LANES:(s + 1) * LANES], jnp.where(at, values[j], 0.0)
            )
    xcopies = [
        copy(xmsg.at[i - 1], xin.at[i - 1], x_s.at[i - 1], x_r.at[i - 1], group(i))
        for i in range(1, n_groups)
    ]
    for item in xcopies:
        item.start()

    keep_leaving(blocks // 8 - 1)
    half = LANES // 2
    low, high = pl.ds(0, half), pl.ds(half, half)
    bulk = [
        copy(leaving.at[1, low], passing.at[0], bulk_s.at[0], bulk_r.at[0], group(1)),
        copy(leaving.at[1, high], passing.at[1], bulk_s.at[1], bulk_r.at[1], group(3)),
        copy(leaving.at[0], arrived.at[0], bulk_s.at[2], bulk_r.at[2], group(1)),
        copy(leaving.at[2], arrived.at[2], bulk_s.at[3], bulk_r.at[3], group(3)),
    ]
    bulk_on = [
        copy(passing.at[0], arrived.at[1, low], bulk_s.at[4], bulk_r.at[4], group(1)),
        copy(passing.at[1], arrived.at[1, high], bulk_s.at[5], bulk_r.at[5], group(3)),
    ]
    for item in xcopies:
        item.wait()
    for item in bulk:
        item.start()
    for s in range(slabs):
        arr[s] = xin[0, s] + xin[1, s] + xin[2, s]
    slab_waits(first_sent, msg, g2, p1_s, p1_r)

    def plane(at, h):
        return g2.at[at, pl.ds(4 * h, 4)]

    def plane_b(at, h):
        return a2.at[at, pl.ds(4 * h, 4)]

    p2 = (along_v, v, plane, p2_s, p2_r)
    p2b = (along_v, v, plane_b, p2b_s, p2b_r)
    sent = ring_start(*p2)
    second_sent = slab_sends(arr, a2, p1b_s, p1b_r)
    slab_waits(second_sent, arr, a2, p1b_s, p1b_r)
    sent_b = ring_start(*p2b)
    sent += ring_relay(*p2)
    sent_b += ring_relay(*p2b)
    for n in range(2):
        bulk[n].wait_recv()
        bulk_on[n].start()
    for n in range(2, 6):
        ring_wait(*p2, n)

    codes = jnp.zeros((8, LANES), jnp.float32)
    for i in range(4):
        for q in range(8):
            codes = codes + g2[i, q, blocks:blocks + 8, :]
    codes = codes.astype(jnp.int32)
    target = iota((lists, LANES), 0)

    def piece(ref, zz, yy, count):
        one = jnp.where(flat, zz, yy)
        two = jnp.where(flat, yy, zz) * 2
        return [ref[one, two, 0:count, :], ref[one, two + 1, 0:count, :]]

    def split(values):
        high = values.astype(jnp.bfloat16)
        low = (values - high.astype(jnp.float32)).astype(jnp.bfloat16)
        return jnp.concatenate([high, low], axis=1)

    def chunk(rows, values):
        slots = [(row >> 8) - 1 for row in rows]
        held = [(row & 255).astype(jnp.float32) for row in rows]
        hot = jnp.concatenate(
            [jnp.where(target == slot, 1.0, 0.0).astype(jnp.bfloat16) for slot in slots], axis=1
        )
        part = jnp.dot(hot, split(values), preferred_element_type=jnp.float32)
        held = jnp.concatenate(held, axis=1)
        held = jnp.broadcast_to(held, (LANES, held.shape[1])).astype(jnp.bfloat16)
        total = lax.dot_general(hot, held, NT, preferred_element_type=jnp.float32)
        return part[:, :LANES] + part[:, LANES:], total

    slab = jnp.zeros((lists, LANES), jnp.float32)
    totals = jnp.zeros((lists, LANES), jnp.float32)
    for zz in range(4):
        values = jnp.concatenate(sum([piece(g2, zz, yy, blocks) for yy in range(4)], []), axis=0)
        part, total = chunk([codes[2 * zz:2 * zz + 1], codes[2 * zz + 1:2 * zz + 2]], values)
        slab, totals = slab + part, totals + total
    for n in range(2, 6):
        ring_wait(*p2b, n)
    codes = jnp.zeros((8, LANES), jnp.float32)
    for i in range(4):
        for q in range(8):
            codes = codes + a2[i, q]
    codes = codes[3:5].astype(jnp.int32)
    values = jnp.concatenate(
        sum([piece(a2, zz, yy, 8) for zz in range(4) for yy in range(4)], []), axis=0
    )
    part, total = chunk([codes[0:1], codes[1:2]], values)
    slab, totals = slab + part, totals + total

    prior_load.wait()
    prior = 1.0 * PRIOR
    table[:, columns(sid)] = (
        (slab + prior * previous[...].astype(jnp.float32)) / (totals + prior)
    ).astype(jnp.bfloat16)

    def part_of(at, h):
        return table.at[pl.ds(h * (lists // 2), lists // 2), columns(core * 4 + at)]

    p3 = (along_u, u, part_of, p3_s, p3_r)
    spread = ring_start(*p3)

    def hand(n, s):
        ref = table.at[:, columns(s)]
        return copy(ref, ref, mate_s.at[n], mate_r.at[n], mate)

    order = (0, 3, 1, 2)
    relays = [hand(n, core * 4 + lax.rem(u + i, 4)) for n, i in enumerate(order)]
    relays[0].start()
    spread += ring_relay(*p3)
    ring_wait(*p3, 2)
    relays[1].start()
    ring_wait(*p3, 3)
    relays[2].start()
    ring_wait(*p3, 4)
    ring_wait(*p3, 5)
    relays[3].start()
    w = jnp.where(flat, z, y)
    for n, i in enumerate(order):
        hand(n, (1 - core) * 4 + lax.rem(w + i, 4)).wait_recv()

    ones = jnp.ones((8, table.shape[1]), jnp.bfloat16)
    squares = jnp.square(table[...].astype(jnp.float32))
    high = squares.astype(jnp.bfloat16)
    low = (squares - high.astype(jnp.float32)).astype(jnp.bfloat16)
    norms = lax.dot_general(ones, high, NT, preferred_element_type=jnp.float32)
    norms = norms + lax.dot_general(ones, low, NT, preferred_element_type=jnp.float32)
    norms_out[...] = norms
    for item in bulk[2:] + bulk_on:
        item.wait_recv()
    for j, out in enumerate((f0, f1, f2)):
        dots = lax.dot_general(arrived[j], table[...], NT, preferred_element_type=jnp.float32)
        out[...] = ((2.0 * dots - norms[0:1]) * factor).astype(jnp.bfloat16)
    for item in bulk + bulk_on + sent + sent_b + spread + relays:
        item.wait_send()


def alive_column(row):
    eye = iota((LANES, LANES), 0) == iota((LANES, LANES), 1)
    return jnp.sum(jnp.where(eye, row, 0.0), axis=1, keepdims=True)


def scores_kernel(cnt, keep, vec, table, norms, bl_hbm, hp_hbm, scores_ref, new_ref, pick_ref,
                  held, bl, hp, sems, small, *, factor, share, sizes, n_groups, n_rows):
    g = lax.axis_index("grp")
    d = lax.axis_index("row")
    tables = [
        pltpu.make_async_copy(src, dst, small.at[i])
        for i, (src, dst) in enumerate(((bl_hbm, bl), (hp_hbm, hp)))
    ]
    for item in tables:
        item.start()
    new_ref[...] = table[pl.ds(pl.multiple_of(d * share, share), share), :]
    lane = iota((1, LANES), 1)
    started, begin = [], 0
    for i, size in enumerate(sizes):
        if i >= 2:
            started[i - 2].wait()
        dots = lax.dot_general(
            vec[begin:begin + size, :], table[...], NT, preferred_element_type=jnp.float32
        )
        for b in range(size // LANES):
            k = begin // LANES + b
            row = jnp.where(lane < cnt[k], keep[k:k + 1, :], 0).astype(jnp.float32)
            held[i % 2, b * LANES:(b + 1) * LANES, :] = (
                (2.0 * dots[b * LANES:(b + 1) * LANES] - norms[0:1]) * factor
            ) * alive_column(row)
        started.append(pltpu.make_async_copy(
            held.at[i % 2, pl.ds(0, size), :], scores_ref.at[pl.ds(begin, size), :], sems.at[i % 2]
        ))
        started[-1].start()
        begin += size
    for item in tables:
        item.wait()
    blocks = keep.shape[0]
    picks = [jnp.int32(-1)] * (n_groups - 1)
    for k in range(blocks):
        home = hp[bl[(g * n_rows + d) * blocks + k]]
        away = lax.rem(home // table.shape[0] - g + n_groups, n_groups)
        picks = [jnp.where(away == j + 1, k, pick) for j, pick in enumerate(picks)]
    for j, pick in enumerate(picks):
        pick_ref[j] = pick
        pick_ref[4 + j] = jnp.maximum(pick, 0)
    for item in started[-2:]:
        item.wait()


def merge_kernel(pick, cnt, keep_ref, b0, b1, b2, _, scores_ref, held, sems):
    lane = iota((1, LANES), 1)
    backs = (b0, b1, b2)

    def put(j):
        first = pl.multiple_of(pick[4 + j] * LANES, LANES)
        return pltpu.make_async_copy(held.at[j], scores_ref.at[pl.ds(first, LANES), :], sems.at[j])

    for j, back in enumerate(backs):
        @pl.when(pick[j] >= 0)
        def _():
            k = pick[4 + j]
            row = jnp.where(lane < cnt[k], keep_ref[pl.ds(k, 1), :], 0).astype(jnp.float32)
            held[j] = back[...].astype(jnp.float32) * alive_column(row)
            put(j).start()
    for j in range(len(backs)):
        @pl.when(pick[j] >= 0)
        def _():
            put(j).wait()


def local(vectors, keep_bits, counts, block_list, home_pos, old_centroids):
    n_groups = lax.axis_size("grp")
    n_rows = lax.axis_size("row")
    blocks = counts.shape[0]
    total_rows, width = vectors.shape
    block_rows = total_rows // blocks
    lists_group = old_centroids.shape[0]
    factor = 1.0 / math.sqrt(width)
    slabs = width // LANES
    away = n_groups - 1
    keep = keep_bits.reshape(blocks, block_rows)
    whole = pl.BlockSpec(memory_space=pltpu.VMEM)
    scalars = pl.BlockSpec(memory_space=pltpu.SMEM)
    there = pl.BlockSpec(memory_space=pl.ANY)
    f32, bf16 = jnp.float32, jnp.bfloat16
    dma = pltpu.SemaphoreType.DMA
    found_shape = pltpu.VMEM((block_rows, lists_group), bf16)
    operands = (
        block_list.reshape(-1, LANES), home_pos.reshape(-1, LANES), counts.reshape(1, blocks),
        keep, vectors, old_centroids,
    )
    vec, table, norms, f0, f1, f2 = pl.pallas_call(
        functools.partial(table_kernel, n_groups=n_groups, n_rows=n_rows, factor=factor),
        out_shape=(
            pltpu.VMEM((total_rows, width), bf16),
            pltpu.VMEM((lists_group, width), bf16),
            pltpu.VMEM((8, lists_group), f32),
            found_shape, found_shape, found_shape,
        ),
        in_specs=[pl.BlockSpec(memory_space=pltpu.HBM)] * 6,
        out_specs=(whole,) * 6,
        scratch_shapes=[
            pltpu.VMEM((block_list.shape[0] // LANES, LANES), jnp.int32),
            pltpu.VMEM((home_pos.shape[0] // LANES, LANES), jnp.int32),
            pltpu.VMEM((1, blocks), jnp.int32),
            pltpu.VMEM((blocks, LANES), jnp.int32),
            pltpu.VMEM((blocks, LANES), f32),
            pltpu.VMEM((blocks, width), f32),
            pltpu.VMEM((slabs, blocks + 8, LANES), f32),
            pltpu.VMEM((away, slabs, 8, LANES), f32),
            pltpu.VMEM((away, block_rows, width), bf16),
            pltpu.VMEM((lists_group, LANES), bf16),
            pltpu.VMEM((away, slabs, 8, LANES), f32),
            pltpu.VMEM((slabs, 8, LANES), f32),
            pltpu.VMEM((4, 8, blocks + 8, LANES), f32),
            pltpu.VMEM((4, 8, 8, LANES), f32),
            pltpu.VMEM((2, block_rows // 2, width), bf16),
            pltpu.VMEM((away, block_rows, width), bf16),
            dma((8,)), dma((5,)),
            dma((8,)), dma((8,)), dma((8,)), dma((8,)),
            dma((3,)), dma((3,)), dma((6,)), dma((6,)),
            dma((6,)), dma((6,)), dma((6,)), dma((6,)), dma((6,)), dma((6,)),
            dma((4,)), dma((4,)),
        ],
        compiler_params=pltpu.CompilerParams(
            collective_id=0, has_side_effects=True, vmem_limit_bytes=24 << 20
        ),
        name="table",
    )(*(pltpu.with_memory_space_constraint(x, pltpu.HBM) for x in operands))

    backs = [
        lax.ppermute(found, "grp", [(s, (s - j - 1) % n_groups) for s in range(n_groups)])
        for j, found in enumerate((f0, f1, f2))
    ]

    sizes = [8 * block_rows] * 3 + [4 * block_rows] * 2
    scores, new_centroids, picks = pl.pallas_call(
        functools.partial(scores_kernel, factor=factor, share=lists_group // n_rows, sizes=sizes,
                          n_groups=n_groups, n_rows=n_rows),
        out_shape=(
            jax.ShapeDtypeStruct((total_rows, lists_group), f32),
            jax.ShapeDtypeStruct((lists_group // n_rows, width), bf16),
            jax.ShapeDtypeStruct((8,), jnp.int32),
        ),
        in_specs=[scalars] + [whole] * 4 + [there] * 2,
        out_specs=(there, whole, scalars),
        scratch_shapes=[
            pltpu.VMEM((2, sizes[0], lists_group), f32),
            pltpu.SMEM(block_list.shape, jnp.int32),
            pltpu.SMEM(home_pos.shape, jnp.int32),
            dma((2,)), dma((2,)),
        ],
        compiler_params=pltpu.CompilerParams(vmem_limit_bytes=24 << 20),
        cost_estimate=pl.CostEstimate(
            flops=2 * total_rows * width * lists_group,
            bytes_accessed=total_rows * 4 * lists_group,
            transcendentals=0,
        ),
        name="scores",
    )(counts, keep, vec, table, norms, block_list, home_pos)

    scores = pl.pallas_call(
        merge_kernel,
        out_shape=jax.ShapeDtypeStruct(scores.shape, f32),
        in_specs=[scalars] * 2 + [whole] * 4 + [there],
        out_specs=there,
        scratch_shapes=[pltpu.VMEM((away, block_rows, lists_group), f32), dma((away,))],
        input_output_aliases={6: 0},
        compiler_params=pltpu.CompilerParams(vmem_limit_bytes=8 << 20),
        name="merge",
    )(picks, counts, keep, *backs, scores)
    return new_centroids, scores


def solution(mesh):
    in_specs = (
        P(("grp", "row"), None),
        P(("grp", "row")),
        P(("grp", "row")),
        P(),
        P(),
        P("grp", None),
    )
    out_specs = (P(("grp", "row"), None), P(("grp", "row"), None))
    return jax.shard_map(local, mesh=mesh, in_specs=in_specs, out_specs=out_specs, check_vma=False)
```

time: 345 us -> 51.4 us (0.15)
  matrix products: 88.5 us -> 0 us
  waiting for transfers between devices: 79.4 us -> 0.24 us
  blocking collectives: 66.9 us -> 0 us
  local copies, waits for them, and re-layouts: 49.8 us -> 0.02 us
  Pallas kernels: 0 us -> 47.3 us
  loops' own time: 20 us -> 0 us
  other arithmetic: 16.7 us -> 0 us
  between operations: 14.2 us -> 0.86 us
  starting transfers between devices: 8.1 us -> 2.95 us
    dot_general x37 -> x0, matrix products: 88.5 us -> none  [the longest x32 80.2 us: score_rows(): lax.dot_general(rows, table, (((1,), (1,)), ((), ())), preferred_element_...]
    psum x1 -> x0, blocking collectives: 66.9 us -> none  [local(): all_sums, all_totals = lax.psum((sums, totals), 'row')]
    pallas_call x0 -> x3, Pallas kernels: none -> 47.3 us  [the longest x1 37.6 us: local(): pl.pallas_call(functools.partial(table_kernel, n_groups=n_groups, n_rows=...]
    all_gather x1 -> x0, waiting for transfers between devices: 39.1 us -> none  [local(): tables = lax.all_gather(table, 'grp', axis=0, tiled=True)]
    psum x1 -> x0, waiting for transfers between devices: 34.9 us -> none  [local(): all_sums, all_totals = lax.psum((sums, totals), 'row')]
    gather x4 -> x0, local copies, waits for them, and re-layouts: 24.9 us -> none  [the longest x1 23 us: local(): homes = jnp.take(home_pos, block_list)]
    dynamic_slice x66 -> x0, local copies, waits for them, and re-layouts: 23.5 us -> none  [the longest x32 19.5 us: local(): scores = lax.map(one_block, (masked, alive, mine_groups))]
    another operation x1 -> x0, loops' own time: 20 us -> none  [local(): scores = lax.map(one_block, (masked, alive, mine_groups))]
  transfers between devices with their start and end apart: 4 -> 3, of which waited for: 4 -> 1; matrix products, arithmetic and copies ran while one was open for 4% -> 0% of each run, Pallas kernels for 0% -> 16%
where the time goes in v2:
time: 51.4 us
  Pallas kernels  47.3 us (92%)
  starting transfers between devices  2.95 us (6%)
  between operations  0.86 us (2%)
    pallas_call x1, Pallas kernels, local(): pl.pallas_call(functools.partial(table_kernel, n_groups=n_groups, n_rows=...  37.6 us
    pallas_call x1, Pallas kernels, local(): pl.pallas_call(functools.partial(scores_kernel, factor=factor, share=list...  8.17 us
    ppermute x3, starting transfers between devices, local(): lax.ppermute(found, 'grp', [(s, (s - j - 1) % n_groups) for s in range(n_...  2.95 us
    pallas_call x1, Pallas kernels, local(): pl.pallas_call(merge_kernel, out_shape=jax.ShapeDtypeStruct(scores.shape,...  1.49 us
  transfers between devices with their start and end apart: 3, of which 1 were waited for; matrix products, arithmetic and copies ran while one was open for 0% of the time, Pallas kernels for 16%

profile of v2, /device:TPU:1, one launch (start us, length us, event | category | flops | bytes accessed | tf_op | source)
XLA Modules:
  0.0 51.4 jit_solution(9930689350421009461)
XLA Ops:
  0.6 0.0 copy-start.1
  0.6 0.0 copy-start.2
  0.7 0.0 copy-start.3
  0.7 0.0 copy-start
  0.7 37.6 %table.1 = (bf16[4096,1024]{1,0:T(8,128)(2,1)S(1)}, bf16[512,1024]{1,0:T(8,128)(2,1)S(1)}, f32[8,512]{1,0:T(8,128)S(1)}, bf16[128,512]{1,0:T(8,128)(2,1)S(1)}, b...) custom-call(s32[32,128]{1,0:T(8,128)} %bitcast.7, s32[16,128]{1,0:T(8,128)} %bitcast.8, s32[1,32]{1,0:T(1,128)} %bitcast.9, ...), custom_call_target="tpu_custom_call" | custom-call | tf_op jit(solution)/shard_map/table/pallas_call | solution.py:460
  38.3 1.7 %collective-permute-start = (bf16[128,512]{1,0:T(8,128)(2,1)S(1)}, bf16[128,512]{1,0:T(8,128)(2,1)S(1)}, u32[]{:S(2)}, u32[]{:S(2)}) collective-permute-start(bf16[128,512]{1,0:T(8,128)(2,1)S(1)} %get-tuple-element.16), channel_id=1, source_target_pairs={{0,96},{32,0},{64,32},{96,64},{1,97},{33,1},{65,33},{97,65},{2,98}... | collective-permute-start | bytes 393224 | tf_op jit(solution)/shard_map/ppermute | solution.py:500
  40.0 0.7 %collective-permute-start.1 = (bf16[128,512]{1,0:T(8,128)(2,1)S(1)}, bf16[128,512]{1,0:T(8,128)(2,1)S(1)}, u32[]{:S(2)}, u32[]{:S(2)}) collective-permute-start(bf16[128,512]{1,0:T(8,128)(2,1)S(1)} %get-tuple-element.17), channel_id=1, source_target_pairs={{0,64},{32,96},{64,0},{96,32},{1,65},{33,97},{65,1},{97,33},{2,66}... | collective-permute-start | bytes 393224 | tf_op jit(solution)/shard_map/ppermute | solution.py:500
  40.7 0.5 %collective-permute-start.2 = (bf16[128,512]{1,0:T(8,128)(2,1)S(1)}, bf16[128,512]{1,0:T(8,128)(2,1)S(1)}, u32[]{:S(2)}, u32[]{:S(2)}) collective-permute-start(bf16[128,512]{1,0:T(8,128)(2,1)S(1)} %get-tuple-element.18), channel_id=1, source_target_pairs={{0,32},{32,64},{64,96},{96,0},{1,33},{33,65},{65,97},{97,1},{2,34}... | collective-permute-start | bytes 393224 | tf_op jit(solution)/shard_map/ppermute | solution.py:500
  41.2 0.0 copy-done.1
  41.2 0.0 copy-done.2
  41.3 0.0 copy-done.3
  41.3 0.0 copy-done
  41.3 8.2 %scores.1 = (f32[4096,512]{1,0:T(8,128)}, bf16[16,1024]{1,0:T(8,128)(2,1)}, s32[8]{0:T(128)S(1)}) custom-call(s32[32]{0:T(128)S(1)} %copy-done.3, s32[32,128]{1,0:T(8,128)S(1)} %bitcast.5, bf16[4096,1024]{1,0:T(8,128)(2,1)S(1)} %get-tuple-element.11.vec, bf16[512,1024]{1,0:T(8,128)(2,1)S(1)} %get-tuple-element.12.table, ...), custom_call_target="tpu_custom_call" | custom-call | flops 4294967296 | bytes 8388608 | tf_op jit(solution)/shard_map/scores/pallas_call | solution.py:505
  49.4 0.0 collective-permute-done.b0
  49.5 0.0 collective-permute-done.1.b1
  49.5 0.2 collective-permute-done.2.b2
  49.7 1.5 %merge.1 = f32[4096,512]{1,0:T(8,128)} custom-call(s32[8]{0:T(128)S(1)} %get-tuple-element.15.pick, s32[32]{0:T(128)S(1)} %copy-done.3, s32[32,128]{1,0:T(8,128)S(1)} %bitcast.6, bf16[128,512]{1,0:T(8,128)(2,1)S(1)} %collective-permute-done.b0, bf16[128,512]{1,0:T(8,128)(2,1)S(1)} %collective-permute-done.1.b1, ...), custom_call_target="tpu_custom_call", output_to_operand_aliasing={{}: (6, {})} | custom-call | tf_op jit(solution)/shard_map/merge/pallas_call | solution.py:530
Async XLA Ops:
  0.6 40.6 %copy-start.1 = (s32[4096]{0:T(1024)S(1)}, s32[4096]{0:T(1024)}, u32[]{:S(2)}) copy-start(s32[4096]{0:T(1024)} %bl_hbm.1) | copy-start | bytes 49156
  0.6 40.6 %copy-start.2 = (s32[2048]{0:T(1024)S(1)}, s32[2048]{0:T(1024)}, u32[]{:S(2)}) copy-start(s32[2048]{0:T(1024)} %hp_hbm.1) | copy-start | bytes 24580
  0.7 40.6 %copy-start.3 = (s32[32]{0:T(128)S(1)}, s32[32]{0:T(128)}, u32[]{:S(2)}) copy-start(s32[32]{0:T(128)} %cnt.3) | copy-start | bytes 388
  0.7 40.6 %copy-start = (s32[4096]{0:T(1024)S(1)}, s32[4096]{0:T(1024)}, u32[]{:S(2)}) copy-start(s32[4096]{0:T(1024)} %param.7) | copy-start | bytes 49156
  38.3 11.2 %collective-permute-start = (bf16[128,512]{1,0:T(8,128)(2,1)S(1)}, bf16[128,512]{1,0:T(8,128)(2,1)S(1)}, u32[]{:S(2)}, u32[]{:S(2)}) collective-permute-start(bf16[128,512]{1,0:T(8,128)(2,1)S(1)} %get-tuple-element.16), channel_id=1, source_target_pairs={{0,96},{32,0},{64,32},{96,64},{1,97},{33,1},{65,33},{97,65},{2,98}... | collective-permute-start | bytes 393224 | tf_op jit(solution)/shard_map/ppermute | solution.py:500
  40.0 9.5 %collective-permute-start.1 = (bf16[128,512]{1,0:T(8,128)(2,1)S(1)}, bf16[128,512]{1,0:T(8,128)(2,1)S(1)}, u32[]{:S(2)}, u32[]{:S(2)}) collective-permute-start(bf16[128,512]{1,0:T(8,128)(2,1)S(1)} %get-tuple-element.17), channel_id=1, source_target_pairs={{0,64},{32,96},{64,0},{96,32},{1,65},{33,97},{65,1},{97,33},{2,66}... | collective-permute-start | bytes 393224 | tf_op jit(solution)/shard_map/ppermute | solution.py:500
  40.7 9.0 %collective-permute-start.2 = (bf16[128,512]{1,0:T(8,128)(2,1)S(1)}, bf16[128,512]{1,0:T(8,128)(2,1)S(1)}, u32[]{:S(2)}, u32[]{:S(2)}) collective-permute-start(bf16[128,512]{1,0:T(8,128)(2,1)S(1)} %get-tuple-element.18), channel_id=1, source_target_pairs={{0,32},{32,64},{64,96},{96,0},{1,33},{33,65},{65,97},{97,1},{2,34}... | collective-permute-start | bytes 393224 | tf_op jit(solution)/shard_map/ppermute | solution.py:500
